TPU v7x, 512 devices: a whole 4x8x8 slice. The times are simulated.
512 devices in a mesh: ctx: 64 (over z, x, core), tp: 8 (over y).
Axes of the slice: x: 4, y: 8, z: 8, core: 2. Of those that a mesh axis runs over, the one named last changes fastest.
Arguments:
- queries: bfloat16 [16384, 8192], P('ctx', 'tp'), may hold values from -8 to 8
- key_heads: bfloat16 [16384, 1024], P('ctx', 'tp'), may hold values from -8 to 8
- value_heads: bfloat16 [16384, 1024], P('ctx', 'tp'), may hold values from -6 to 6
- out_grad: bfloat16 [16384, 8192], P(('ctx', 'tp')), may hold values from -6 to 6
- doc_lengths: int32 [32], replicated, may hold values from 1 to 9, 128 in all
Outputs:
- grad_queries: bfloat16 [16384, 8192], P('ctx', 'tp')
- grad_keys: bfloat16 [16384, 1024], P('ctx', 'tp')
- grad_values: bfloat16 [16384, 1024], P('ctx', 'tp')
Inputs may be any that keep to these rules, and one draw needn't show every extreme that they name: `doc_lengths`: documents fill the window in order, whole blocks of 128 rows each; the lengths sum to 128 and the longest is exactly 9.
All inputs are finite; a program needn't handle non-finite values.
Results may differ from a plain program's by a relative error of at most 0.009.
Values may be sent and summed in bfloat16 or wider, within the bound.
A program may use at most 64 MiB of HBM per device.

v0:
```python
import jax
import jax.numpy as jnp
from jax import lax
from jax.sharding import PartitionSpec as P

HD = 128
GROUP = 8
BLK = 128
REACH = 4


def passed_along(block, axis, distance):
    devices = range(lax.axis_size(axis))
    route = [(i - distance, i) for i in devices if i - distance in devices]
    return lax.ppermute(block, axis, route)


def body(queries, key_heads, value_heads, out_grad, doc_lengths):
    rows_here = queries.shape[0]
    head_pairs = key_heads.shape[1] // HD
    score_scale = HD ** (-0.5)
    position = lax.axis_index("ctx")
    first_row = position * rows_here
    doc_ends = jnp.cumsum(doc_lengths) * BLK
    offsets = jnp.arange(rows_here, dtype=jnp.int32)
    grad_here = lax.all_to_all(out_grad, "tp", split_axis=1, concat_axis=0, tiled=True)
    query_split = queries.reshape(rows_here, head_pairs, GROUP, HD)
    grads_split = grad_here.reshape(rows_here, head_pairs, GROUP, HD)

    def visible(query_first, key_first):
        query_rows = query_first + offsets
        key_rows = key_first + offsets
        query_docs = jnp.sum((query_rows[:, None] >= doc_ends[None, :]).astype(jnp.int32), axis=1)
        key_docs = jnp.sum((key_rows[:, None] >= doc_ends[None, :]).astype(jnp.int32), axis=1)
        return (
            (query_docs[:, None] == key_docs[None, :])
            & (key_rows[None, :] <= query_rows[:, None])
            & (key_rows[None, :] >= 0)
        )

    def masked_scores(query_block, key_block, allowed):
        raw = jnp.einsum(
            "rkgd,ckd->kgrc", query_block, key_block, preferred_element_type=jnp.float32
        )
        return jnp.where(allowed, raw * score_scale, -jnp.inf)

    def prob_grads(grad_block, value_block):
        return jnp.einsum(
            "rkgd,ckd->kgrc", grad_block, value_block, preferred_element_type=jnp.float32
        )

    neighbours = [(key_heads, value_heads)]
    for distance in range(1, REACH + 1):
        neighbours.append(passed_along((key_heads, value_heads), "ctx", distance))
    shaped = [
        (pair[0].reshape(rows_here, head_pairs, HD), pair[1].reshape(rows_here, head_pairs, HD))
        for pair in neighbours
    ]
    allowed_list = [
        visible(first_row, first_row - distance * rows_here) for distance in range(REACH + 1)
    ]
    active = [jnp.any(allowed) for allowed in allowed_list]

    def stat_update(key_block, value_block, allowed, row_max, row_sum, row_dot):
        scores = masked_scores(query_split, key_block, allowed)
        grad_prob = prob_grads(grads_split, value_block)
        updated = jnp.maximum(row_max, jnp.max(scores, axis=-1))
        factor = jnp.exp(row_max - updated)
        lifted = jnp.exp(scores - updated[..., None])
        row_sum = row_sum * factor + jnp.sum(lifted, axis=-1)
        row_dot = row_dot * factor + jnp.sum(lifted * grad_prob, axis=-1)
        return (updated, row_sum, row_dot)

    def keep_stats(key_block, value_block, allowed, row_max, row_sum, row_dot):
        return (row_max, row_sum, row_dot)

    row_max = jnp.full((head_pairs, GROUP, rows_here), -jnp.inf, jnp.float32)
    row_sum = jnp.zeros((head_pairs, GROUP, rows_here), jnp.float32)
    row_dot = jnp.zeros((head_pairs, GROUP, rows_here), jnp.float32)
    for distance in range(REACH + 1):
        row_max, row_sum, row_dot = lax.cond(
            active[distance],
            stat_update,
            keep_stats,
            shaped[distance][0],
            shaped[distance][1],
            allowed_list[distance],
            row_max,
            row_sum,
            row_dot,
        )
    log_total = row_max + jnp.log(row_sum)
    grad_dot = row_dot / row_sum

    def full_step(key_block, value_block, allowed):
        scores = masked_scores(query_split, key_block, allowed)
        weights = jnp.exp(scores - log_total[..., None])
        grad_prob = prob_grads(grads_split, value_block)
        value_term = jnp.einsum(
            "kgrc,rkgd->ckd",
            weights.astype(jnp.bfloat16),
            grads_split,
            preferred_element_type=jnp.float32,
        )
        dscore = (weights * (grad_prob - grad_dot[..., None])).astype(jnp.bfloat16)
        query_term = (
            jnp.einsum("kgrc,ckd->rkgd", dscore, key_block, preferred_element_type=jnp.float32)
            * score_scale
        )
        key_term = (
            jnp.einsum("kgrc,rkgd->ckd", dscore, query_split, preferred_element_type=jnp.float32)
            * score_scale
        )
        return (
            query_term,
            key_term.reshape(rows_here, head_pairs * HD),
            value_term.reshape(rows_here, head_pairs * HD),
        )

    def skip_step(key_block, value_block, allowed):
        return (
            jnp.zeros((rows_here, head_pairs, GROUP, HD), jnp.float32),
            jnp.zeros((rows_here, head_pairs * HD), jnp.float32),
            jnp.zeros((rows_here, head_pairs * HD), jnp.float32),
        )

    query_total = jnp.zeros((rows_here, head_pairs, GROUP, HD), jnp.float32)
    key_parts = []
    value_parts = []
    for distance in range(REACH + 1):
        query_term, key_term, value_term = lax.cond(
            active[distance],
            full_step,
            skip_step,
            shaped[distance][0],
            shaped[distance][1],
            allowed_list[distance],
        )
        query_total = query_total + query_term
        key_parts.append(key_term)
        value_parts.append(value_term)
    key_total = key_parts[0]
    value_total = value_parts[0]
    for distance in range(1, REACH + 1):
        arrived = (
            passed_along(key_parts[distance].astype(jnp.bfloat16), "ctx", -distance).astype(
                jnp.float32
            ),
            passed_along(value_parts[distance].astype(jnp.bfloat16), "ctx", -distance).astype(
                jnp.float32
            ),
        )
        key_total = key_total + arrived[0]
        value_total = value_total + arrived[1]
    return (
        query_total.reshape(rows_here, head_pairs * GROUP * HD).astype(jnp.bfloat16),
        key_total.astype(jnp.bfloat16),
        value_total.astype(jnp.bfloat16),
    )


def solution(mesh):
    placed = (P("ctx", "tp"), P("ctx", "tp"), P("ctx", "tp"), P(("ctx", "tp"), None), P())
    return jax.shard_map(
        body,
        mesh=mesh,
        in_specs=placed,
        out_specs=(P("ctx", "tp"), P("ctx", "tp"), P("ctx", "tp")),
        check_vma=False,
    )
```

profile of v0, /device:TPU:449, one launch (start us, length us, event | category | flops | bytes accessed | tf_op | source)
XLA Modules:
  0.0 120.3 jit_solution(15700705875513901989)
XLA Ops:
  0.7 3.3 %collective-permute-start.2 = (bf16[256,128]{1,0:T(8,128)(2,1)}, bf16[256,128]{1,0:T(8,128)(2,1)S(1)}, u32[]{:S(2)}, u32[]{:S(2)}) collective-permute-start(bf16[256,128]{1,0:T(8,128)(2,1)} %param.26), channel_id=1, source_target_pairs={{0,16},{8,24},{16,32},{24,40},{32,48},{40,56},{48,64},{56,72},{64,... | collective-permute-start | bytes 196616 | tf_op jit(solution)/shard_map/ppermute | solution.py:15
  3.9 4.0 %collective-permute-start = (bf16[256,128]{1,0:T(8,128)(2,1)}, bf16[256,128]{1,0:T(8,128)(2,1)S(1)}, u32[]{:S(2)}, u32[]{:S(2)}) collective-permute-start(bf16[256,128]{1,0:T(8,128)(2,1)} %param.26), channel_id=1, source_target_pairs={{0,8},{8,16},{16,24},{24,32},{32,40},{40,48},{48,56},{56,64},{64,7... | collective-permute-start | bytes 196616 | tf_op jit(solution)/shard_map/ppermute | solution.py:15
  7.9 2.3 %collective-permute-start.6 = (bf16[256,128]{1,0:T(8,128)(2,1)}, bf16[256,128]{1,0:T(8,128)(2,1)S(1)}, u32[]{:S(2)}, u32[]{:S(2)}) collective-permute-start(bf16[256,128]{1,0:T(8,128)(2,1)} %param.26), channel_id=1, source_target_pairs={{0,32},{8,40},{16,48},{24,56},{32,64},{40,72},{48,80},{56,88},{64,... | collective-permute-start | bytes 196616 | tf_op jit(solution)/shard_map/ppermute | solution.py:15
  10.2 2.1 %collective-permute-start.4 = (bf16[256,128]{1,0:T(8,128)(2,1)}, bf16[256,128]{1,0:T(8,128)(2,1)S(1)}, u32[]{:S(2)}, u32[]{:S(2)}) collective-permute-start(bf16[256,128]{1,0:T(8,128)(2,1)} %param.26), channel_id=1, source_target_pairs={{0,24},{8,32},{16,40},{24,48},{32,56},{40,64},{48,72},{56,80},{64,... | collective-permute-start | bytes 196616 | tf_op jit(solution)/shard_map/ppermute | solution.py:15
  12.4 1.9 %collective-permute-start.1 = (bf16[256,128]{1,0:T(8,128)(2,1)}, bf16[256,128]{1,0:T(8,128)(2,1)S(1)}, u32[]{:S(2)}, u32[]{:S(2)}) collective-permute-start(bf16[256,128]{1,0:T(8,128)(2,1)} %param.27), channel_id=1, source_target_pairs={{0,8},{8,16},{16,24},{24,32},{32,40},{40,48},{48,56},{56,64},{64,7... | collective-permute-start | bytes 196616 | tf_op jit(solution)/shard_map/ppermute | solution.py:15
  14.3 1.9 %copy.144 = bf16[4,8,8,1024]{3,2,0,1:T(8,128)(2,1)} copy(bf16[4,8,8,1024]{3,2,1,0:T(8,128)(2,1)} %bitcast.534) | data formatting | bytes 1048576 | tf_op jit(solution)/shard_map/all_to_all | solution.py:26
  16.2 7.0 %all-to-all-start = ((bf16[32,8,1024]{2,0,1:T(8,128)(2,1)}), bf16[32,8,1024]{2,0,1:T(8,128)(2,1)S(1)}, u32[]{:S(2)}, u32[]{:S(2)}) async-start(bf16[32,8,1024]{2,0,1:T(8,128)(2,1)} %bitcast.511), calls=%async_computation | async-start | bytes 1048576 | tf_op jit(solution)/shard_map/all_to_all | solution.py:26
  23.6 2.2 %collective-permute-start.3 = (bf16[256,128]{1,0:T(8,128)(2,1)S(1)}, bf16[256,128]{1,0:T(8,128)(2,1)}, u32[]{:S(2)}, u32[]{:S(2)}) collective-permute-start(bf16[256,128]{1,0:T(8,128)(2,1)S(1)} %copy-done.4), channel_id=1, source_target_pairs={{0,16},{8,24},{16,32},{24,40},{32,48},{40,56},{48,64},{56,72},{64,... | collective-permute-start | bytes 196616 | tf_op jit(solution)/shard_map/ppermute | solution.py:15
  25.8 1.9 %collective-permute-start.7 = (bf16[256,128]{1,0:T(8,128)(2,1)S(1)}, bf16[256,128]{1,0:T(8,128)(2,1)S(1)}, u32[]{:S(2)}, u32[]{:S(2)}) collective-permute-start(bf16[256,128]{1,0:T(8,128)(2,1)S(1)} %copy-done.4), channel_id=1, source_target_pairs={{0,32},{8,40},{16,48},{24,56},{32,64},{40,72},{48,80},{56,88},{64,... | collective-permute-start | bytes 196616 | tf_op jit(solution)/shard_map/ppermute | solution.py:15
  27.8 1.9 %collective-permute-start.5 = (bf16[256,128]{1,0:T(8,128)(2,1)S(1)}, bf16[256,128]{1,0:T(8,128)(2,1)}, u32[]{:S(2)}, u32[]{:S(2)}) collective-permute-start(bf16[256,128]{1,0:T(8,128)(2,1)S(1)} %copy-done.4), channel_id=1, source_target_pairs={{0,24},{8,32},{16,40},{24,48},{32,56},{40,64},{48,72},{56,80},{64,... | collective-permute-start | bytes 196616 | tf_op jit(solution)/shard_map/ppermute | solution.py:15
  29.7 2.1 %and_and_fusion.4 = (pred[256,256]{0,1:T(8,128)(4,1)}, pred[]{:T(512)}, pred[]{:T(512)}, pred[256,256]{0,1:T(8,128)(4,1)S(1)}, pred[]{:T(512)}, /*index=5*/pred[...) fusion(s32[256]{0:T(256)S(1)} %iota_add_fusion.4, ...), kind=kLoop, calls=%fused_computation.191 | loop fusion | flops 1638395 | bytes 339205 | tf_op jit(solution)/shard_map/and | solution.py:36
  35.0 4.9 %all-to-all-done = bf16[32,8,1024]{2,0,1:T(8,128)(2,1)S(1)} async-done(((bf16[32,8,1024]{2,0,1:T(8,128)(2,1)}), bf16[32,8,1024]{2,0,1:T(8,128)(2,1)S(1)}, u32[]{:S(2)}, u32[]{:S(2)}) %all-to-all-start) | async-done | bytes 524320 | tf_op jit(solution)/shard_map/all_to_all | solution.py:26
  40.0 4.8 %conditional.10 = (f32[1,8,256]{2,1,0:T(8,128)}, f32[1,8,256]{2,1,0:T(8,128)S(1)}, f32[1,8,256]{2,1,0:T(8,128)S(1)}) conditional(s32[]{:T(128)} %convert_element_type.131, () %tuple.103, (pred[256,256]{0,1:T(8,128)(4,1)}, bf16[256,1,128]{2,0,1:T(8,128)(2,1)S(1)}, bf16[256,1,8,128]{0,3,2,1:T(8,128)(2,1)S(1)}, bf16[256,1,128]{2,0,1:T(8,128)(2,1)S(1)}, ...), branch_computations={%region_11.12_spmd, %region_12.16_spmd} | conditional | flops 272631808 | bytes 7618584 | solution.py:81
  40.0 1.9 %fusion.130 = (f32[8,256]{1,0:T(8,128)}, f32[1,8,256,256]{2,3,1,0:T(8,128)S(1)}) fusion(bf16[256,1,8,128]{0,3,2,1:T(8,128)(2,1)S(1)} %get-tuple-element.449, bf16[256,1,128]{2,0,1:T(8,128)(2,1)S(1)} %get-tuple-element.219, pred[256,256]{0,1:T(8,128)(4,1)} %get-tuple-element.218), kind=kOutput, calls=%fused_computation.216 | convolution fusion | flops 135788544 | bytes 2760704 | tf_op jit(solution)/shard_map/cond/branch_1_fun/rkgd,ckd->kgrc/dot_general | solution.py:42
  41.9 1.2 %fusion = f32[8,256]{1,0:T(8,128)S(1)} fusion(f32[1,8,256,256]{2,3,1,0:T(8,128)S(1)} %get-tuple-element.538, f32[8,256]{1,0:T(8,128)} %get-tuple-element.537, bf16[256,1,8,128]{3,2,0,1:T(8,128)(2,1)S(1)} %get-tuple-element.451, bf16[256,1,128]{2,0,1:T(8,128)(2,1)S(1)} %get-tuple-element.221), kind=kOutput, calls=%fused_computation.1 | convolution fusion | flops 135788544 | bytes 2703360 | tf_op jit(solution)/shard_map/cond/branch_1_fun/rkgd,ckd->kgrc/dot_general | solution.py:48
  43.1 1.0 fusion.1
  44.8 4.1 %conditional.11 = ((f32[1,8,256]{2,1,0:T(8,128)}, f32[1,8,256]{2,1,0:T(8,128)S(1)}, f32[1,8,256]{2,1,0:T(8,128)S(1)})) conditional(s32[]{:T(128)} %convert_element_type.139, (f32[1,8,256]{2,1,0:T(8,128)}, f32[1,8,256]{2,1,0:T(8,128)S(1)}, f32[1,8,256]{2,1,0:T(8,128)S(1)}) %conditional.10, (pred[256,256]{0,1:T(8,128)(4,1)}, ...), branch_computations={%region_16.17_spmd, %region_17.21_spmd} | conditional | flops 272635904 | bytes 7684128 | solution.py:81
  44.8 1.3 %fusion.131 = (f32[8,256]{1,0:T(8,128)S(1)}, f32[1,8,256,256]{2,3,1,0:T(8,128)S(1)}) fusion(bf16[256,1,8,128]{0,3,2,1:T(8,128)(2,1)S(1)} %get-tuple-element.454, bf16[256,1,128]{2,0,1:T(8,128)(2,1)S(1)} %get-tuple-element.225, pred[256,256]{0,1:T(8,128)(4,1)} %get-tuple-element.224), kind=kOutput, calls=%fused_computation.217 | convolution fusion | flops 135788544 | bytes 2760704 | tf_op jit(solution)/shard_map/cond/branch_1_fun/rkgd,ckd->kgrc/dot_general | solution.py:42
  47.7 0.7 bitcast_add_fusion.2
  49.0 4.1 %conditional.12 = ((f32[1,8,256]{2,1,0:T(8,128)}, f32[1,8,256]{2,1,0:T(8,128)S(1)}, f32[1,8,256]{2,1,0:T(8,128)S(1)})) conditional(s32[]{:T(128)} %convert_element_type.137, (f32[1,8,256]{2,1,0:T(8,128)}, f32[1,8,256]{2,1,0:T(8,128)S(1)}, f32[1,8,256]{2,1,0:T(8,128)S(1)}) %get-tuple-element.635, (pred[256,256]{0,1:T(8,128)(4,1)S(1)}, ...), branch_computations={%region_21.22_spmd, %region_22.26_spmd} | conditional | flops 272635904 | bytes 7684128 | solution.py:81
  50.1 1.4 %fusion.14 = f32[8,256]{1,0:T(8,128)S(1)} fusion(f32[1,8,256,256]{2,3,1,0:T(8,128)S(1)} %get-tuple-element.546, f32[8,256]{1,0:T(8,128)S(1)} %bitcast.559, bf16[256,1,8,128]{3,2,0,1:T(8,128)(2,1)S(1)} %get-tuple-element.467, bf16[256,1,128]{2,0,1:T(8,128)(2,1)} %get-tuple-element.237), kind=kOutput, calls=%fused_computation.28 | convolution fusion | flops 135788544 | bytes 2703360 | tf_op jit(solution)/shard_map/cond/branch_1_fun/rkgd,ckd->kgrc/dot_general | solution.py:48
  51.8 0.7 bitcast_add_fusion.4
  53.2 0.7 fusion.135
  53.9 1.3 %conditional.19 = (f32[256,1,8,128]{3,0,2,1:T(8,128)S(1)}, bf16[256,128]{1,0:T(8,128)(2,1)}, bf16[256,128]{1,0:T(8,128)(2,1)}) conditional(s32[]{:T(128)} %convert_element_type.133, () %tuple.116, (pred[256,256]{0,1:T(8,128)(4,1)S(1)}, bf16[256,1,128]{2,0,1:T(8,128)(2,1)S(1)}, bf16[256,1,8,128]{0,3,2,1:T(8,128)(2,1)S(1)}, ...), branch_computations={%region_44.45_spmd, %region_45.46_spmd} | conditional | flops 675086336 | bytes 12992536 | solution.py:131
  55.2 1.9 %collective-permute-start.11 = (bf16[256,128]{1,0:T(8,128)(2,1)}, bf16[256,128]{1,0:T(8,128)(2,1)}, u32[]{:S(2)}, u32[]{:S(2)}) collective-permute-start(bf16[256,128]{1,0:T(8,128)(2,1)} %get-tuple-element.347), channel_id=1, source_target_pairs={{32,0},{40,8},{48,16},{56,24},{64,32},{72,40},{80,48},{88,56},{96,... | collective-permute-start | bytes 196616 | tf_op jit(solution)/shard_map/ppermute | solution.py:15
  57.1 5.2 %collective-permute-start.15 = (bf16[256,128]{1,0:T(8,128)(2,1)}, bf16[256,128]{1,0:T(8,128)(2,1)}, u32[]{:S(2)}, u32[]{:S(2)}) collective-permute-start(bf16[256,128]{1,0:T(8,128)(2,1)} %get-tuple-element.352), channel_id=1, source_target_pairs={{32,0},{40,8},{48,16},{56,24},{64,32},{72,40},{80,48},{88,56},{96,... | collective-permute-start | bytes 196616 | tf_op jit(solution)/shard_map/ppermute | solution.py:15
  62.4 4.1 %conditional.16 = (f32[256,1,8,128]{3,0,2,1:T(8,128)S(1)}, bf16[256,128]{1,0:T(8,128)(2,1)S(1)}, bf16[256,128]{1,0:T(8,128)(2,1)}) conditional(s32[]{:T(128)} %convert_element_type.139, () %tuple.110, (pred[256,256]{0,1:T(8,128)(4,1)}, bf16[256,1,128]{2,0,1:T(8,128)(2,1)S(1)}, bf16[256,1,8,128]{0,3,2,1:T(8,128)(2,1)S(1)}, ...), branch_computations={%region_38.39_spmd, %region_39.40_spmd} | conditional | flops 675086336 | bytes 12992536 | solution.py:131
  62.6 1.4 %fusion.49 = f32[1,8,256,256]{2,3,1,0:T(8,128)S(1)} fusion(f32[8,256]{1,0:T(8,128)S(1)} %bitcast.566, pred[256,256]{0,1:T(8,128)(4,1)} %get-tuple-element.262, bf16[256,1,8,128]{0,3,2,1:T(8,128)(2,1)S(1)} %get-tuple-element.493, bf16[256,1,128]{2,0,1:T(8,128)(2,1)S(1)} %get-tuple-element.263), kind=kOutput, calls=%fused_computation.83 | convolution fusion | flops 135790592 | bytes 2760704 | tf_op jit(solution)/shard_map/cond/branch_1_fun/rkgd,ckd->kgrc/dot_general | solution.py:42
  64.0 1.1 convolution_bitcast_fusion.2
  66.5 3.0 %collective-permute-start.12 = (bf16[256,128]{1,0:T(8,128)(2,1)}, bf16[256,128]{1,0:T(8,128)(2,1)}, u32[]{:S(2)}, u32[]{:S(2)}) collective-permute-start(bf16[256,128]{1,0:T(8,128)(2,1)} %get-tuple-element.349), channel_id=1, source_target_pairs={{8,0},{16,8},{24,16},{32,24},{40,32},{48,40},{56,48},{64,56},{72,6... | collective-permute-start | bytes 196616 | tf_op jit(solution)/shard_map/ppermute | solution.py:15
  69.5 4.7 %conditional.17 = (f32[256,1,8,128]{3,0,2,1:T(8,128)S(1)}, bf16[256,128]{1,0:T(8,128)(2,1)S(1)}, bf16[256,128]{1,0:T(8,128)(2,1)}) conditional(s32[]{:T(128)} %convert_element_type.137, () %tuple.112, (pred[256,256]{0,1:T(8,128)(4,1)}, bf16[256,1,128]{2,0,1:T(8,128)(2,1)S(1)}, bf16[256,1,8,128]{0,3,2,1:T(8,128)(2,1)S(1)}, ...), branch_computations={%region_40.41_spmd, %region_41.42_spmd} | conditional | flops 675086336 | bytes 12992536 | solution.py:131
  69.5 1.4 %fusion.67 = f32[1,8,256,256]{2,3,1,0:T(8,128)S(1)} fusion(f32[8,256]{1,0:T(8,128)S(1)} %bitcast.567, pred[256,256]{0,1:T(8,128)(4,1)} %get-tuple-element.269, bf16[256,1,8,128]{0,3,2,1:T(8,128)(2,1)S(1)} %get-tuple-element.500, bf16[256,1,128]{2,0,1:T(8,128)(2,1)S(1)} %get-tuple-element.270), kind=kOutput, calls=%fused_computation.106 | convolution fusion | flops 135790592 | bytes 2760704 | tf_op jit(solution)/shard_map/cond/branch_1_fun/rkgd,ckd->kgrc/dot_general | solution.py:42
  70.9 1.1 convolution_bitcast_fusion.4
  72.0 1.3 %fusion.68 = bf16[8,256,256]{1,2,0:T(8,128)(2,1)S(1)} fusion(f32[1,8,256,256]{2,3,1,0:T(8,128)S(1)} %fusion.67, f32[8,256]{1,0:T(8,128)S(1)} %bitcast.538, bf16[256,1,8,128]{3,2,0,1:T(8,128)(2,1)S(1)} %get-tuple-element.503, bf16[256,1,128]{2,0,1:T(8,128)(2,1)} %get-tuple-element.273), kind=kOutput, calls=%fused_computation.107 | convolution fusion | flops 135790592 | bytes 3743744 | tf_op jit(solution)/shard_map/cond/branch_1_fun/rkgd,ckd->kgrc/dot_general | solution.py:48
  74.3 6.1 %collective-permute-start.13 = (bf16[256,128]{1,0:T(8,128)(2,1)}, bf16[256,128]{1,0:T(8,128)(2,1)}, u32[]{:S(2)}, u32[]{:S(2)}) collective-permute-start(bf16[256,128]{1,0:T(8,128)(2,1)} %get-tuple-element.350), channel_id=1, source_target_pairs={{16,0},{24,8},{32,16},{40,24},{48,32},{56,40},{64,48},{72,56},{80,... | collective-permute-start | bytes 196616 | tf_op jit(solution)/shard_map/ppermute | solution.py:15
  80.4 0.7 conditional.18
  81.2 2.1 %collective-permute-start.14 = (bf16[256,128]{1,0:T(8,128)(2,1)}, bf16[256,128]{1,0:T(8,128)(2,1)}, u32[]{:S(2)}, u32[]{:S(2)}) collective-permute-start(bf16[256,128]{1,0:T(8,128)(2,1)} %get-tuple-element.351), channel_id=1, source_target_pairs={{24,0},{32,8},{40,16},{48,24},{56,32},{64,40},{72,48},{80,56},{88,... | collective-permute-start | bytes 196616 | tf_op jit(solution)/shard_map/ppermute | solution.py:15
  83.4 4.3 %conditional.15 = (f32[256,1,8,128]{3,0,2,1:T(8,128)}, f32[256,128]{1,0:T(8,128)S(1)}, f32[256,128]{1,0:T(8,128)S(1)}) conditional(s32[]{:T(128)} %convert_element_type.131, () %tuple.102, (pred[256,256]{0,1:T(8,128)(4,1)}, bf16[256,1,128]{2,0,1:T(8,128)(2,1)S(1)}, bf16[256,1,8,128]{0,3,2,1:T(8,128)(2,1)S(1)}, f32[1,8,256]{2,1,0:T(8,128)S(1)}, ...), branch_computations={%region_36.37_spmd, %region_37.38_spmd} | conditional | flops 675053568 | bytes 13123608 | solution.py:131
  83.4 1.4 %fusion.31 = f32[1,8,256,256]{2,3,1,0:T(8,128)S(1)} fusion(f32[8,256]{1,0:T(8,128)S(1)} %bitcast.569, pred[256,256]{0,1:T(8,128)(4,1)} %get-tuple-element.255, bf16[256,1,8,128]{0,3,2,1:T(8,128)(2,1)S(1)} %get-tuple-element.486, bf16[256,1,128]{2,0,1:T(8,128)(2,1)S(1)} %get-tuple-element.256), kind=kOutput, calls=%fused_computation.60 | convolution fusion | flops 135790592 | bytes 2760704 | tf_op jit(solution)/shard_map/cond/branch_1_fun/rkgd,ckd->kgrc/dot_general | solution.py:42
  86.1 1.5 %fusion.33 = f32[256,1,8,128]{3,0,2,1:T(8,128)} fusion(bf16[8,256,256]{1,2,0:T(8,128)(2,1)S(1)} %fusion.32, bf16[256,1,128]{2,0,1:T(8,128)(2,1)S(1)} %get-tuple-element.256), kind=kOutput, calls=%fused_computation.63 | convolution fusion | flops 134479872 | bytes 2162688 | tf_op jit(solution)/shard_map/cond/branch_1_fun/kgrc,ckd->rkgd/dot_general | solution.py:107
  87.6 2.1 %add_convert_fusion = bf16[256,1,8,128]{3,0,2,1:T(8,128)(2,1)S(1)} fusion(f32[256,1,8,128]{3,0,2,1:T(8,128)S(1)} %get-tuple-element.342, f32[256,1,8,128]{3,0,2,1:T(8,128)} %copy-done.1, f32[256,1,8,128]{3,0,2,1:T(8,128)} %copy-done, f32[256,1,8,128]{3,0,2,1:T(8,128)} %get-tuple-element.338, f32[256,1,8,128]{3,0,2,1:T(8,128)S(1)} %get-tuple-element.339), kind=kLoop, calls=%fused_computation.184 | loop fusion | flops 1310720 | bytes 5767168 | tf_op jit(solution)/shard_map/convert_element_type | solution.py:156
  90.1 0.9 copy.143
  91.0 15.0 %collective-permute-start.8 = (bf16[256,128]{1,0:T(8,128)(2,1)S(1)}, bf16[256,128]{1,0:T(8,128)(2,1)S(1)}, u32[]{:S(2)}, u32[]{:S(2)}) collective-permute-start(bf16[256,128]{1,0:T(8,128)(2,1)S(1)} %copy-done.9), channel_id=1, source_target_pairs={{8,0},{16,8},{24,16},{32,24},{40,32},{48,40},{56,48},{64,56},{72,6... | collective-permute-start | bytes 196616 | tf_op jit(solution)/shard_map/ppermute | solution.py:15
  106.0 5.7 %collective-permute-start.9 = (bf16[256,128]{1,0:T(8,128)(2,1)S(1)}, bf16[256,128]{1,0:T(8,128)(2,1)S(1)}, u32[]{:S(2)}, u32[]{:S(2)}) collective-permute-start(bf16[256,128]{1,0:T(8,128)(2,1)S(1)} %copy-done.11), channel_id=1, source_target_pairs={{16,0},{24,8},{32,16},{40,24},{48,32},{56,40},{64,48},{72,56},{80,... | collective-permute-start | bytes 196616 | tf_op jit(solution)/shard_map/ppermute | solution.py:15
  111.7 1.9 %collective-permute-start.10 = (bf16[256,128]{1,0:T(8,128)(2,1)S(1)}, bf16[256,128]{1,0:T(8,128)(2,1)S(1)}, u32[]{:S(2)}, u32[]{:S(2)}) collective-permute-start(bf16[256,128]{1,0:T(8,128)(2,1)S(1)} %copy-done.13), channel_id=1, source_target_pairs={{24,0},{32,8},{40,16},{48,24},{56,32},{64,40},{72,48},{80,56},{88,... | collective-permute-start | bytes 196616 | tf_op jit(solution)/shard_map/ppermute | solution.py:15
  113.7 1.6 %add_convert_fusion.1 = bf16[256,128]{1,0:T(8,128)(2,1)} fusion(bf16[256,128]{1,0:T(8,128)(2,1)} %collective-permute-done.15, bf16[256,128]{1,0:T(8,128)(2,1)} %collective-permute-done.14, bf16[256,128]{1,0:T(8,128)(2,1)} %collective-permute-done.13, f32[256,128]{1,0:T(8,128)S(1)} %get-tuple-element.348, bf16[256,128]{1,0:T(8,128)(2,1)} %collective-permute-done.12), kind=kLoop, calls=%fused_computation.192 | loop fusion | flops 294912 | bytes 458752 | tf_op jit(solution)/shard_map/convert_element_type | solution.py:158
  115.3 3.5 %collective-permute-done.10 = bf16[256,128]{1,0:T(8,128)(2,1)S(1)} collective-permute-done((bf16[256,128]{1,0:T(8,128)(2,1)S(1)}, bf16[256,128]{1,0:T(8,128)(2,1)S(1)}, u32[]{:S(2)}, u32[]{:S(2)}) %collective-permute-start.10) | collective-permute-done | bytes 65568 | tf_op jit(solution)/shard_map/ppermute | solution.py:15
  118.8 1.5 %add_convert_fusion.2 = bf16[256,128]{1,0:T(8,128)(2,1)} fusion(bf16[256,128]{1,0:T(8,128)(2,1)} %collective-permute-done.11, bf16[256,128]{1,0:T(8,128)(2,1)S(1)} %collective-permute-done.10, bf16[256,128]{1,0:T(8,128)(2,1)S(1)} %collective-permute-done.9, f32[256,128]{1,0:T(8,128)S(1)} %get-tuple-element.343, bf16[256,128]{1,0:T(8,128)(2,1)S(1)} %collective-permute-done.8), kind=kLoop, calls=%fused_computation.193 | loop fusion | flops 294912 | bytes 458752 | tf_op jit(solution)/shard_map/convert_element_type | solution.py:157
  (83 shorter events, 11.7 us)
Async XLA Ops:
  0.6 23.0 %copy-start.4 = (bf16[256,128]{1,0:T(8,128)(2,1)S(1)}, bf16[256,128]{1,0:T(8,128)(2,1)}, u32[]{:S(2)}) copy-start(bf16[256,128]{1,0:T(8,128)(2,1)} %param.27) | copy-start | bytes 196612
  0.6 22.5 %copy-start.14 = (s32[32]{0:T(128)S(1)}, s32[32]{0:T(128)}, u32[]{:S(2)}) copy-start(s32[32]{0:T(128)} %param.29) | copy-start | bytes 388
  0.7 34.1 %copy-start.2 = (bf16[256,1024]{1,0:T(8,128)(2,1)S(1)}, bf16[256,1024]{1,0:T(8,128)(2,1)}, u32[]{:S(2)}) copy-start(bf16[256,1024]{1,0:T(8,128)(2,1)} %param.25) | copy-start | bytes 1572868
  0.7 22.9 %collective-permute-start.2 = (bf16[256,128]{1,0:T(8,128)(2,1)}, bf16[256,128]{1,0:T(8,128)(2,1)S(1)}, u32[]{:S(2)}, u32[]{:S(2)}) collective-permute-start(bf16[256,128]{1,0:T(8,128)(2,1)} %param.26), channel_id=1, source_target_pairs={{0,16},{8,24},{16,32},{24,40},{32,48},{40,56},{48,64},{56,72},{64,... | collective-permute-start | bytes 196616 | tf_op jit(solution)/shard_map/ppermute | solution.py:15
  3.9 21.9 %collective-permute-start = (bf16[256,128]{1,0:T(8,128)(2,1)}, bf16[256,128]{1,0:T(8,128)(2,1)S(1)}, u32[]{:S(2)}, u32[]{:S(2)}) collective-permute-start(bf16[256,128]{1,0:T(8,128)(2,1)} %param.26), channel_id=1, source_target_pairs={{0,8},{8,16},{16,24},{24,32},{32,40},{40,48},{48,56},{56,64},{64,7... | collective-permute-start | bytes 196616 | tf_op jit(solution)/shard_map/ppermute | solution.py:15
  7.9 45.2 %collective-permute-start.6 = (bf16[256,128]{1,0:T(8,128)(2,1)}, bf16[256,128]{1,0:T(8,128)(2,1)S(1)}, u32[]{:S(2)}, u32[]{:S(2)}) collective-permute-start(bf16[256,128]{1,0:T(8,128)(2,1)} %param.26), channel_id=1, source_target_pairs={{0,32},{8,40},{16,48},{24,56},{32,64},{40,72},{48,80},{56,88},{64,... | collective-permute-start | bytes 196616 | tf_op jit(solution)/shard_map/ppermute | solution.py:15
  10.2 42.9 %collective-permute-start.4 = (bf16[256,128]{1,0:T(8,128)(2,1)}, bf16[256,128]{1,0:T(8,128)(2,1)S(1)}, u32[]{:S(2)}, u32[]{:S(2)}) collective-permute-start(bf16[256,128]{1,0:T(8,128)(2,1)} %param.26), channel_id=1, source_target_pairs={{0,24},{8,32},{16,40},{24,48},{32,56},{40,64},{48,72},{56,80},{64,... | collective-permute-start | bytes 196616 | tf_op jit(solution)/shard_map/ppermute | solution.py:15
  12.4 15.4 %collective-permute-start.1 = (bf16[256,128]{1,0:T(8,128)(2,1)}, bf16[256,128]{1,0:T(8,128)(2,1)S(1)}, u32[]{:S(2)}, u32[]{:S(2)}) collective-permute-start(bf16[256,128]{1,0:T(8,128)(2,1)} %param.27), channel_id=1, source_target_pairs={{0,8},{8,16},{16,24},{24,32},{32,40},{40,48},{48,56},{56,64},{64,7... | collective-permute-start | bytes 196616 | tf_op jit(solution)/shard_map/ppermute | solution.py:15
  16.2 23.8 %copy-start.3 = (bf16[256,128]{1,0:T(8,128)(2,1)S(1)}, bf16[256,128]{1,0:T(8,128)(2,1)}, u32[]{:S(2)}) copy-start(bf16[256,128]{1,0:T(8,128)(2,1)} %param.26) | copy-start | bytes 196612
  16.2 23.7 %all-to-all-start = ((bf16[32,8,1024]{2,0,1:T(8,128)(2,1)}), bf16[32,8,1024]{2,0,1:T(8,128)(2,1)S(1)}, u32[]{:S(2)}, u32[]{:S(2)}) async-start(bf16[32,8,1024]{2,0,1:T(8,128)(2,1)} %bitcast.511), calls=%async_computation | async-start | bytes 1048576 | tf_op jit(solution)/shard_map/all_to_all | solution.py:26
  23.6 25.4 %collective-permute-start.3 = (bf16[256,128]{1,0:T(8,128)(2,1)S(1)}, bf16[256,128]{1,0:T(8,128)(2,1)}, u32[]{:S(2)}, u32[]{:S(2)}) collective-permute-start(bf16[256,128]{1,0:T(8,128)(2,1)S(1)} %copy-done.4), channel_id=1, source_target_pairs={{0,16},{8,24},{16,32},{24,40},{32,48},{40,56},{48,64},{56,72},{64,... | collective-permute-start | bytes 196616 | tf_op jit(solution)/shard_map/ppermute | solution.py:15
  25.8 27.3 %collective-permute-start.7 = (bf16[256,128]{1,0:T(8,128)(2,1)S(1)}, bf16[256,128]{1,0:T(8,128)(2,1)S(1)}, u32[]{:S(2)}, u32[]{:S(2)}) collective-permute-start(bf16[256,128]{1,0:T(8,128)(2,1)S(1)} %copy-done.4), channel_id=1, source_target_pairs={{0,32},{8,40},{16,48},{24,56},{32,64},{40,72},{48,80},{56,88},{64,... | collective-permute-start | bytes 196616 | tf_op jit(solution)/shard_map/ppermute | solution.py:15
  27.8 25.3 %collective-permute-start.5 = (bf16[256,128]{1,0:T(8,128)(2,1)S(1)}, bf16[256,128]{1,0:T(8,128)(2,1)}, u32[]{:S(2)}, u32[]{:S(2)}) collective-permute-start(bf16[256,128]{1,0:T(8,128)(2,1)S(1)} %copy-done.4), channel_id=1, source_target_pairs={{0,24},{8,32},{16,40},{24,48},{32,56},{40,64},{48,72},{56,80},{64,... | collective-permute-start | bytes 196616 | tf_op jit(solution)/shard_map/ppermute | solution.py:15
  31.8 17.2 %copy-start.7 = (pred[256,256]{0,1:T(8,128)(4,1)}, pred[256,256]{0,1:T(8,128)(4,1)S(1)}, u32[]{:S(2)}) copy-start(pred[256,256]{0,1:T(8,128)(4,1)S(1)} %get-tuple-element.560) | copy-start | bytes 196612
  31.8 21.3 %copy-start.5 = (pred[256,256]{0,1:T(8,128)(4,1)}, pred[256,256]{0,1:T(8,128)(4,1)S(1)}, u32[]{:S(2)}) copy-start(pred[256,256]{0,1:T(8,128)(4,1)S(1)} %get-tuple-element.564) | copy-start | bytes 196612
  55.2 60.1 %collective-permute-start.11 = (bf16[256,128]{1,0:T(8,128)(2,1)}, bf16[256,128]{1,0:T(8,128)(2,1)}, u32[]{:S(2)}, u32[]{:S(2)}) collective-permute-start(bf16[256,128]{1,0:T(8,128)(2,1)} %get-tuple-element.347), channel_id=1, source_target_pairs={{32,0},{40,8},{48,16},{56,24},{64,32},{72,40},{80,48},{88,56},{96,... | collective-permute-start | bytes 196616 | tf_op jit(solution)/shard_map/ppermute | solution.py:15
  57.1 33.9 %collective-permute-start.15 = (bf16[256,128]{1,0:T(8,128)(2,1)}, bf16[256,128]{1,0:T(8,128)(2,1)}, u32[]{:S(2)}, u32[]{:S(2)}) collective-permute-start(bf16[256,128]{1,0:T(8,128)(2,1)} %get-tuple-element.352), channel_id=1, source_target_pairs={{32,0},{40,8},{48,16},{56,24},{64,32},{72,40},{80,48},{88,56},{96,... | collective-permute-start | bytes 196616 | tf_op jit(solution)/shard_map/ppermute | solution.py:15
  66.4 3.1 %copy-start.8 = (bf16[256,128]{1,0:T(8,128)(2,1)}, bf16[256,128]{1,0:T(8,128)(2,1)S(1)}, u32[]{:S(2)}) copy-start(bf16[256,128]{1,0:T(8,128)(2,1)S(1)} %get-tuple-element.344) | copy-start | bytes 196612
  66.5 7.8 %copy-start.6 = (pred[256,256]{0,1:T(8,128)(4,1)S(1)}, pred[256,256]{0,1:T(8,128)(4,1)}, u32[]{:S(2)}) copy-start(pred[256,256]{0,1:T(8,128)(4,1)} %copy-done.5) | copy-start | bytes 196612
  66.5 39.6 %collective-permute-start.12 = (bf16[256,128]{1,0:T(8,128)(2,1)}, bf16[256,128]{1,0:T(8,128)(2,1)}, u32[]{:S(2)}, u32[]{:S(2)}) collective-permute-start(bf16[256,128]{1,0:T(8,128)(2,1)} %get-tuple-element.349), channel_id=1, source_target_pairs={{8,0},{16,8},{24,16},{32,24},{40,32},{48,40},{56,48},{64,56},{72,6... | collective-permute-start | bytes 196616 | tf_op jit(solution)/shard_map/ppermute | solution.py:15
  74.2 6.2 %copy-start = (f32[256,1,8,128]{3,0,2,1:T(8,128)}, f32[256,1,8,128]{3,0,2,1:T(8,128)S(1)}, u32[]{:S(2)}) copy-start(f32[256,1,8,128]{3,0,2,1:T(8,128)S(1)} %get-tuple-element.340) | copy-start | bytes 3145732
  74.2 6.2 %copy-start.10 = (bf16[256,128]{1,0:T(8,128)(2,1)}, bf16[256,128]{1,0:T(8,128)(2,1)S(1)}, u32[]{:S(2)}) copy-start(bf16[256,128]{1,0:T(8,128)(2,1)S(1)} %get-tuple-element.345) | copy-start | bytes 196612
  74.3 37.5 %collective-permute-start.13 = (bf16[256,128]{1,0:T(8,128)(2,1)}, bf16[256,128]{1,0:T(8,128)(2,1)}, u32[]{:S(2)}, u32[]{:S(2)}) collective-permute-start(bf16[256,128]{1,0:T(8,128)(2,1)} %get-tuple-element.350), channel_id=1, source_target_pairs={{16,0},{24,8},{32,16},{40,24},{48,32},{56,40},{64,48},{72,56},{80,... | collective-permute-start | bytes 196616 | tf_op jit(solution)/shard_map/ppermute | solution.py:15
  81.2 2.2 %copy-start.12 = (bf16[256,128]{1,0:T(8,128)(2,1)}, bf16[256,128]{1,0:T(8,128)(2,1)S(1)}, u32[]{:S(2)}) copy-start(bf16[256,128]{1,0:T(8,128)(2,1)S(1)} %get-tuple-element.346) | copy-start | bytes 196612
  81.2 2.2 %copy-start.1 = (f32[256,1,8,128]{3,0,2,1:T(8,128)}, f32[256,1,8,128]{3,0,2,1:T(8,128)S(1)}, u32[]{:S(2)}) copy-start(f32[256,1,8,128]{3,0,2,1:T(8,128)S(1)} %get-tuple-element.341) | copy-start | bytes 3145732
  81.2 32.5 %collective-permute-start.14 = (bf16[256,128]{1,0:T(8,128)(2,1)}, bf16[256,128]{1,0:T(8,128)(2,1)}, u32[]{:S(2)}, u32[]{:S(2)}) collective-permute-start(bf16[256,128]{1,0:T(8,128)(2,1)} %get-tuple-element.351), channel_id=1, source_target_pairs={{24,0},{32,8},{40,16},{48,24},{56,32},{64,40},{72,48},{80,56},{88,... | collective-permute-start | bytes 196616 | tf_op jit(solution)/shard_map/ppermute | solution.py:15
  89.8 1.3 %copy-start.9 = (bf16[256,128]{1,0:T(8,128)(2,1)S(1)}, bf16[256,128]{1,0:T(8,128)(2,1)}, u32[]{:S(2)}) copy-start(bf16[256,128]{1,0:T(8,128)(2,1)} %copy-done.8) | copy-start | bytes 196612
  89.8 16.3 %copy-start.11 = (bf16[256,128]{1,0:T(8,128)(2,1)S(1)}, bf16[256,128]{1,0:T(8,128)(2,1)}, u32[]{:S(2)}) copy-start(bf16[256,128]{1,0:T(8,128)(2,1)} %copy-done.10) | copy-start | bytes 196612
  89.8 22.0 %copy-start.13 = (bf16[256,128]{1,0:T(8,128)(2,1)S(1)}, bf16[256,128]{1,0:T(8,128)(2,1)}, u32[]{:S(2)}) copy-start(bf16[256,128]{1,0:T(8,128)(2,1)} %copy-done.12) | copy-start | bytes 196612
  91.0 24.3 %collective-permute-start.8 = (bf16[256,128]{1,0:T(8,128)(2,1)S(1)}, bf16[256,128]{1,0:T(8,128)(2,1)S(1)}, u32[]{:S(2)}, u32[]{:S(2)}) collective-permute-start(bf16[256,128]{1,0:T(8,128)(2,1)S(1)} %copy-done.9), channel_id=1, source_target_pairs={{8,0},{16,8},{24,16},{32,24},{40,32},{48,40},{56,48},{64,56},{72,6... | collective-permute-start | bytes 196616 | tf_op jit(solution)/shard_map/ppermute | solution.py:15
  106.0 9.3 %collective-permute-start.9 = (bf16[256,128]{1,0:T(8,128)(2,1)S(1)}, bf16[256,128]{1,0:T(8,128)(2,1)S(1)}, u32[]{:S(2)}, u32[]{:S(2)}) collective-permute-start(bf16[256,128]{1,0:T(8,128)(2,1)S(1)} %copy-done.11), channel_id=1, source_target_pairs={{16,0},{24,8},{32,16},{40,24},{48,32},{56,40},{64,48},{72,56},{80,... | collective-permute-start | bytes 196616 | tf_op jit(solution)/shard_map/ppermute | solution.py:15
  111.7 7.1 %collective-permute-start.10 = (bf16[256,128]{1,0:T(8,128)(2,1)S(1)}, bf16[256,128]{1,0:T(8,128)(2,1)S(1)}, u32[]{:S(2)}, u32[]{:S(2)}) collective-permute-start(bf16[256,128]{1,0:T(8,128)(2,1)S(1)} %copy-done.13), channel_id=1, source_target_pairs={{24,0},{32,8},{40,16},{48,24},{56,32},{64,40},{72,48},{80,56},{88,... | collective-permute-start | bytes 196616 | tf_op jit(solution)/shard_map/ppermute | solution.py:15
where the time goes:
time: 122 us; the launch traced here: 120 us
  starting transfers between devices  67.6 us (55%)
  matrix products  19.4 us (16%)
  other arithmetic  13.5 us (11%)
  waiting for transfers between devices  8.5 us (7%)
  local copies, waits for them, and re-layouts  6.78 us (6%)
  between operations  4.12 us (3%)
    ppermute x16, starting transfers between devices, passed_along(): return lax.ppermute(block, axis, route)  60.7 us
    dot_general x6, matrix products, masked_scores(): jnp.einsum('rkgd,ckd->kgrc', query_block, key_block, preferred_element_ty...  7.83 us
    all_to_all x1, starting transfers between devices, body(): lax.all_to_all(out_grad, 'tp', split_axis=1, concat_axis=0, tiled=True)  6.95 us
    dot_general x6, matrix products, prob_grads(): jnp.einsum('rkgd,ckd->kgrc', grad_block, value_block, preferred_element_t...  5.26 us
    all_to_all x1, waiting for transfers between devices, body(): lax.all_to_all(out_grad, 'tp', split_axis=1, concat_axis=0, tiled=True)  4.93 us
    ppermute x16, waiting for transfers between devices, passed_along(): return lax.ppermute(block, axis, route)  3.57 us
    dot_general x3, matrix products, full_step(): jnp.einsum('kgrc,rkgd->ckd', weights.astype(jnp.bfloat16), grads_split, p...  2.57 us
    dot_general x3, matrix products, full_step(): jnp.einsum('kgrc,ckd->rkgd', dscore, key_block, preferred_element_type=jn...  2.45 us
  transfers between devices with their start and end apart: 17, of which 2 were waited for; matrix products, arithmetic and copies ran while one was open for 30% of the time, Pallas kernels for 0%

commit v1 on v0

v1 whole, which is shorter than its diff:
```python
import functools

import jax
import jax.numpy as jnp
from jax import lax
from jax.experimental import pallas as pl
from jax.experimental.pallas import tpu as pltpu
from jax.sharding import PartitionSpec as P

HD = 128
GROUP = 8
BLK = 128
REACH = 4
ROWS = 256
CHUNKS = REACH + 1
BIG = 1e30
FLOOR = -1e29
SCALE = HD ** (-0.5)
LOG2E = 1.4426950408889634
MESH = pl.DeviceIdType.MESH
NT = (((1,), (1,)), ((), ()))
NN = (((1,), (0,)), ((), ()))


def mm(a, b, dims):
    return lax.dot_general(a, b, dims, preferred_element_type=jnp.float32)


def kernel(n_ctx, n_tp, lengths, queries, key_heads, value_heads, out_grad, dq_out, dk_out, dv_out,
           q, keys, values, keys_t, grads, probs, dprobs, top, total, factor, hide, dkey, dvalue, dq,
           send_k, send_v, got_k, got_v, own_k, own_v,
           q_sem, kv_own_sem, k_recv, v_recv, kv_send, g_recv, g_send, c_send, ck_recv, cv_recv, dq_sem, out_sem):
    i = lax.axis_index("ctx")
    t = lax.axis_index("tp")

    def q_copy(h):
        return pltpu.make_async_copy(queries.at[:, pl.ds(h * HD, HD)], q.at[h], q_sem)

    for h in range(GROUP):
        q_copy(h).start()
    k_own = pltpu.make_async_copy(key_heads, keys.at[pl.ds(REACH * ROWS, ROWS)], kv_own_sem.at[0])
    v_own = pltpu.make_async_copy(value_heads, values.at[pl.ds(REACH * ROWS, ROWS)], kv_own_sem.at[1])
    k_own.start()
    v_own.start()

    barrier = pltpu.get_barrier_semaphore()
    for d in range(1, n_tp):
        pl.semaphore_signal(barrier, inc=1, device_id={"tp": lax.rem(t + d, n_tp)}, device_id_type=MESH)
    for d in range(1, REACH + 1):
        @pl.when(i >= d)
        def _():
            pl.semaphore_signal(barrier, inc=1, device_id={"ctx": i - d}, device_id_type=MESH)

        @pl.when(i + d < n_ctx)
        def _():
            pl.semaphore_signal(barrier, inc=1, device_id={"ctx": i + d}, device_id_type=MESH)

    def scan_doc(k, carry):
        end, first0, first1 = carry
        end = end + lengths[k]
        first0 = jnp.where(end <= 2 * i, jnp.maximum(first0, end), first0)
        first1 = jnp.where(end <= 2 * i + 1, jnp.maximum(first1, end), first1)
        return end, first0, first1

    _, first0, first1 = lax.fori_loop(0, lengths.shape[0], scan_doc, (jnp.int32(0), jnp.int32(0), jnp.int32(0)))
    lane = lax.broadcasted_iota(jnp.int32, (1, ROWS), 1)
    first = jnp.where(lane < BLK, first0, first1)
    last = jnp.where(lane < BLK, 2 * i, 2 * i + 1)
    for j in range(2 * CHUNKS):
        block = 2 * i - 2 * REACH + j
        hide[pl.ds(j, 1), :] = jnp.where((block >= first) & (block <= last), 0.0, BIG)
    for j in range(REACH):
        @pl.when(i < REACH - j)
        def _():
            keys[pl.ds(j * ROWS, ROWS), :] = jnp.zeros((ROWS, HD), jnp.bfloat16)
            values[pl.ds(j * ROWS, ROWS), :] = jnp.zeros((ROWS, HD), jnp.bfloat16)
    dkey[...] = jnp.zeros_like(dkey)
    dvalue[...] = jnp.zeros_like(dvalue)

    partners = n_tp - 1 + jnp.minimum(i, REACH) + jnp.minimum(n_ctx - 1 - i, REACH)
    pl.semaphore_wait(barrier, partners)

    def kv_copy(d, what):
        src, dst, recv = ((key_heads, keys, k_recv), (value_heads, values, v_recv))[what]
        return pltpu.make_async_remote_copy(
            src_ref=src, dst_ref=dst.at[pl.ds((REACH - d) * ROWS, ROWS)], send_sem=kv_send.at[d - 1, what],
            recv_sem=recv.at[REACH - d], device_id={"ctx": i + d}, device_id_type=MESH)

    def kv_start(what):
        for d in range(1, REACH + 1):
            @pl.when(i + d < n_ctx)
            def _():
                kv_copy(d, what).start()

    def grad_copy(h, peer):
        return pltpu.make_async_remote_copy(
            src_ref=out_grad.at[:, pl.ds(pl.multiple_of(peer * (GROUP * HD) + h * HD, HD), HD)],
            dst_ref=grads.at[h, pl.ds(t * (ROWS // n_tp), ROWS // n_tp)],
            send_sem=g_send, recv_sem=g_recv.at[h], device_id={"tp": peer}, device_id_type=MESH)

    def grad_start(h):
        for d in (4, 3, 5, 2, 6, 1, 7):
            grad_copy(h, lax.rem(t + d, n_tp)).start()
        pltpu.make_async_copy(
            out_grad.at[:, pl.ds(pl.multiple_of(t * (GROUP * HD) + h * HD, HD), HD)],
            grads.at[h, pl.ds(t * (ROWS // n_tp), ROWS // n_tp)], g_recv.at[h]).start()

    kv_start(0)
    grad_start(0)
    grad_start(1)
    kv_start(1)

    def grads_on(h, carry):
        grad_start(h)
        return carry

    lax.fori_loop(2, GROUP, grads_on, 0)

    pltpu.make_async_copy(q, q, q_sem).wait()
    k_own.wait()

    def scores(j, own):
        rows = pl.ds(j * ROWS, ROWS) if own else pl.ds(pl.multiple_of(j * ROWS, ROWS), ROWS)
        key = keys[rows, :]
        keys_t[j] = key.T
        hide0, hide1 = hide[pl.ds(2 * j, 1), :], hide[pl.ds(2 * j + 1, 1), :]

        def head(h, carry):
            raw = mm(key, q[h], NT) * (SCALE * LOG2E)
            if own:
                row_k = lax.broadcasted_iota(jnp.int32, (ROWS, ROWS), 0)
                row_q = lax.broadcasted_iota(jnp.int32, (ROWS, ROWS), 1)
                raw = jnp.where(row_k <= row_q, raw, -BIG)
            high0 = jnp.max(raw[:BLK], axis=0, keepdims=True) - hide0
            high1 = jnp.max(raw[BLK:], axis=0, keepdims=True) - hide1
            high = jnp.maximum(jnp.maximum(high0, high1), FLOOR)
            e0 = jnp.exp2(raw[:BLK] - (high + hide0))
            e1 = jnp.exp2(raw[BLK:] - (high + hide1))
            top[j, pl.ds(h, 1), :] = high
            total[j, pl.ds(h, 1), :] = jnp.sum(e0, axis=0, keepdims=True) + jnp.sum(e1, axis=0, keepdims=True)
            probs[h, j, :BLK, :] = e0.astype(jnp.bfloat16)
            probs[h, j, BLK:, :] = e1.astype(jnp.bfloat16)
            return carry

        lax.fori_loop(0, GROUP, head, 0)

    scores(REACH, True)

    def far(step, carry):
        j = REACH - 1 - step

        @pl.when(i >= REACH - j)
        def _():
            at = keys.at[pl.ds(pl.multiple_of(j * ROWS, ROWS), ROWS)]
            pltpu.make_async_copy(at, at, k_recv.at[j]).wait()

        scores(j, False)
        return carry

    lax.fori_loop(0, REACH, far, 0)

    highest = jnp.max(top[...], axis=0)
    lifted = [jnp.exp2(top[j] - highest) for j in range(CHUNKS)]
    inverse = 1.0 / sum(lifted[j] * total[j] for j in range(CHUNKS))
    for j in range(CHUNKS):
        factor[j] = lifted[j] * inverse

    v_own.wait()
    for j in range(REACH):
        @pl.when(i >= REACH - j)
        def _():
            at = values.at[pl.ds(j * ROWS, ROWS)]
            pltpu.make_async_copy(at, at, v_recv.at[j]).wait()

    def backward(h, carry):
        pltpu.make_async_copy(grads.at[h], grads.at[h], g_recv.at[h]).wait()
        grad = grads[h]
        query = q[h]
        dots = jnp.zeros((1, ROWS), jnp.float32)
        for j in range(CHUNKS):
            dp = mm(values[pl.ds(j * ROWS, ROWS), :], grad, NT)
            p = probs[h, j].astype(jnp.float32) * factor[j, pl.ds(h, 1), :]
            dots = dots + jnp.sum(p * dp, axis=0, keepdims=True)
            dprobs[j] = dp
            pb = p.astype(jnp.bfloat16)
            probs[h, j] = pb
            rows = pl.ds(j * ROWS, ROWS)
            dvalue[rows, :] += mm(pb, grad, NN)
        dq_t = jnp.zeros((HD, ROWS), jnp.float32)
        for j in range(CHUNKS):
            rows = pl.ds(j * ROWS, ROWS)
            ds = (probs[h, j].astype(jnp.float32) * (dprobs[j] - dots)).astype(jnp.bfloat16)
            dkey[rows, :] += mm(ds, query, NN)
            dq_t = dq_t + mm(keys_t[j], ds, NN)
        dq[h] = (dq_t.T * SCALE).astype(jnp.bfloat16)
        return carry

    lax.fori_loop(0, GROUP, backward, 0)

    def part_copy(d, what):
        src, dst, recv = ((send_k, got_k, ck_recv), (send_v, got_v, cv_recv))[what]
        return pltpu.make_async_remote_copy(
            src_ref=src.at[d - 1], dst_ref=dst.at[d - 1], send_sem=c_send.at[d - 1, what],
            recv_sem=recv.at[d - 1], device_id={"ctx": i - d}, device_id_type=MESH)

    for d in range(REACH, 0, -1):
        rows = pl.ds((REACH - d) * ROWS, ROWS)
        send_k[d - 1] = (dkey[rows, :] * SCALE).astype(jnp.bfloat16)
        send_v[d - 1] = dvalue[rows, :].astype(jnp.bfloat16)

        @pl.when(i >= d)
        def _():
            part_copy(d, 0).start()
            part_copy(d, 1).start()

    for h in range(GROUP):
        pltpu.make_async_copy(dq.at[h], dq_out.at[:, pl.ds(h * HD, HD)], dq_sem).start()

    rows = pl.ds(REACH * ROWS, ROWS)
    dkey[rows, :] = dkey[rows, :] * SCALE
    for d in range(1, REACH + 1):
        @pl.when(i + d < n_ctx)
        def _():
            part_copy(d, 0).wait_recv()
            dkey[rows, :] += got_k[d - 1].astype(jnp.float32)
            part_copy(d, 1).wait_recv()
            dvalue[rows, :] += got_v[d - 1].astype(jnp.float32)
    own_k[...] = dkey[rows, :].astype(jnp.bfloat16)
    own_v[...] = dvalue[rows, :].astype(jnp.bfloat16)
    k_back = pltpu.make_async_copy(own_k, dk_out, out_sem.at[0])
    v_back = pltpu.make_async_copy(own_v, dv_out, out_sem.at[1])
    k_back.start()
    v_back.start()

    for d in range(1, REACH + 1):
        @pl.when(i + d < n_ctx)
        def _():
            kv_copy(d, 0).wait_send()
            kv_copy(d, 1).wait_send()

        @pl.when(i >= d)
        def _():
            part_copy(d, 0).wait_send()
            part_copy(d, 1).wait_send()
    sent = grads.at[pl.ds(0, n_tp - 1)]
    pltpu.make_async_copy(sent, sent, g_send).wait()
    pltpu.make_async_copy(dq, dq, dq_sem).wait()
    k_back.wait()
    v_back.wait()


def body(n_ctx, n_tp, queries, key_heads, value_heads, out_grad, doc_lengths):
    bf, f32 = jnp.bfloat16, jnp.float32
    any_space = pl.BlockSpec(memory_space=pl.ANY)
    dma = pltpu.SemaphoreType.DMA
    return pl.pallas_call(
        functools.partial(kernel, n_ctx, n_tp),
        out_shape=(jax.ShapeDtypeStruct(queries.shape, bf), jax.ShapeDtypeStruct(key_heads.shape, bf),
                   jax.ShapeDtypeStruct(value_heads.shape, bf)),
        in_specs=[pl.BlockSpec(memory_space=pltpu.SMEM)] + [any_space] * 4,
        out_specs=[any_space] * 3,
        scratch_shapes=[
            pltpu.VMEM((GROUP, ROWS, HD), bf),
            pltpu.VMEM((CHUNKS * ROWS, HD), bf),
            pltpu.VMEM((CHUNKS * ROWS, HD), bf),
            pltpu.VMEM((CHUNKS, HD, ROWS), bf),
            pltpu.VMEM((GROUP, ROWS, HD), bf),
            pltpu.VMEM((GROUP, CHUNKS, ROWS, ROWS), bf),
            pltpu.VMEM((CHUNKS, ROWS, ROWS), f32),
            pltpu.VMEM((CHUNKS, GROUP, ROWS), f32),
            pltpu.VMEM((CHUNKS, GROUP, ROWS), f32),
            pltpu.VMEM((CHUNKS, GROUP, ROWS), f32),
            pltpu.VMEM((16, ROWS), f32),
            pltpu.VMEM((CHUNKS * ROWS, HD), f32),
            pltpu.VMEM((CHUNKS * ROWS, HD), f32),
            pltpu.VMEM((GROUP, ROWS, HD), bf),
            pltpu.VMEM((REACH, ROWS, HD), bf),
            pltpu.VMEM((REACH, ROWS, HD), bf),
            pltpu.VMEM((REACH, ROWS, HD), bf),
            pltpu.VMEM((REACH, ROWS, HD), bf),
            pltpu.VMEM((ROWS, HD), bf),
            pltpu.VMEM((ROWS, HD), bf),
            dma, dma((2,)), dma((REACH,)), dma((REACH,)), dma((REACH, 2)), dma((GROUP,)), dma, dma((REACH, 2)),
            dma((REACH,)), dma((REACH,)), dma, dma((2,)),
        ],
        compiler_params=pltpu.CompilerParams(collective_id=0, has_side_effects=True, vmem_limit_bytes=56 << 20),
    )(doc_lengths, queries, key_heads, value_heads, out_grad)


def solution(mesh):
    placed = (P("ctx", "tp"), P("ctx", "tp"), P("ctx", "tp"), P(("ctx", "tp"), None), P())
    return jax.shard_map(
        functools.partial(body, mesh.shape["ctx"], mesh.shape["tp"]),
        mesh=mesh,
        in_specs=placed,
        out_specs=(P("ctx", "tp"), P("ctx", "tp"), P("ctx", "tp")),
        check_vma=False,
    )
```

time: 122 us -> 49.8 us (0.41)
  the two profiles are of different devices: /device:TPU:449 before, /device:TPU:199 now
where the time goes in v1:
time: 49.8 us; the launch traced here: 49.6 us
  Pallas kernels  45.5 us (91%)
  local copies, waits for them, and re-layouts  3.4 us (7%)
  between operations  0.65 us (1%)
    pallas_call x1, Pallas kernels, body(): pl.pallas_call(functools.partial(kernel, n_ctx, n_tp), out_shape=(jax.Sha...  45.5 us
    unnamed x7, local copies, waits for them, and re-layouts  3.4 us

profile of v1, /device:TPU:199, one launch (start us, length us, event | category | flops | bytes accessed | tf_op | source)
XLA Modules:
  0.0 49.6 jit_solution(9696306228286575829)
XLA Ops:
  0.6 45.5 %shard_map.76 = (bf16[256,1024]{1,0:T(8,128)(2,1)}, bf16[256,128]{1,0:T(8,128)(2,1)}, bf16[256,128]{1,0:T(8,128)(2,1)}) custom-call(s32[32]{0:T(128)} %lengths.1, bf16[256,1024]{1,0:T(8,128)(2,1)} %queries.1, bf16[256,128]{1,0:T(8,128)(2,1)} %key_heads.1, bf16[256,128]{1,0:T(8,128)(2,1)} %value_heads.1, bf16[32,8192]{1,0:T(8,128)(2,1)} %out_grad.1), custom_call_target="tpu_custom_call" | custom-call | tf_op jit(solution)/shard_map/pallas_call | solution.py:256
  46.2 0.0 copy-start.1
  46.2 1.9 %copy.11 = bf16[256,1024]{1,0:T(8,128)(2,1)} copy(bf16[256,1024]{1,0:T(8,128)(2,1)} %get-tuple-element.6) | data formatting | bytes 1048576
  48.1 0.0 copy-done.1
  48.1 0.0 copy-start
  48.1 0.6 %copy.12 = bf16[256,128]{1,0:T(8,128)(2,1)} copy(bf16[256,128]{1,0:T(8,128)(2,1)S(1)} %copy-done.1) | data formatting | bytes 131072
  48.7 0.2 copy-done
  48.9 0.6 %copy.13 = bf16[256,128]{1,0:T(8,128)(2,1)} copy(bf16[256,128]{1,0:T(8,128)(2,1)S(1)} %copy-done) | data formatting | bytes 131072
Async XLA Ops:
  46.2 1.9 %copy-start.1 = (bf16[256,128]{1,0:T(8,128)(2,1)S(1)}, bf16[256,128]{1,0:T(8,128)(2,1)}, u32[]{:S(2)}) copy-start(bf16[256,128]{1,0:T(8,128)(2,1)} %get-tuple-element.7) | copy-start | bytes 196612
  48.1 0.9 %copy-start = (bf16[256,128]{1,0:T(8,128)(2,1)S(1)}, bf16[256,128]{1,0:T(8,128)(2,1)}, u32[]{:S(2)}) copy-start(bf16[256,128]{1,0:T(8,128)(2,1)} %get-tuple-element.8) | copy-start | bytes 196612

commit v2 on v1

v2 whole, which is shorter than its diff:
```python
import functools

import jax
import jax.numpy as jnp
from jax import lax
from jax.experimental import pallas as pl
from jax.experimental.pallas import tpu as pltpu
from jax.sharding import PartitionSpec as P

HD = 128
GROUP = 8
BLK = 128
REACH = 4
ROWS = 256
CHUNKS = REACH + 1
BATCH = 4
BIG = 1e30
FLOOR = -1e29
SCALE = HD ** (-0.5)
MESH = pl.DeviceIdType.MESH
NT = (((1,), (1,)), ((), ()))
NN = (((1,), (0,)), ((), ()))


def mm(a, b, dims=NN):
    return lax.dot_general(a, b, dims, preferred_element_type=jnp.float32)


def block(j):
    return pl.ds(j * ROWS if isinstance(j, int) else pl.multiple_of(j * ROWS, ROWS), ROWS)


def kernel(n_ctx, n_tp, lengths, queries, key_heads, value_heads, out_grad, dq, dkv,
           q, keys, values, keys_t, values_t, grads, probs, outs, top, total, factor, hide, dkey, dvalue,
           swap, swapped, part, got, q_sem, own_sem, k_recv, v_recv, kv_send, fwd_send, g_recv, g_send,
           swap_send, swap_recv, part_send, part_recv):
    i = lax.axis_index("ctx")
    t = lax.axis_index("tp")
    odd = lax.rem(i, 2)
    even = odd == 0
    partner = i + 1 - 2 * odd

    for h in range(GROUP):
        pltpu.make_async_copy(queries.at[:, pl.ds(h * HD, HD)], q.at[h], q_sem).start()
    k_own = pltpu.make_async_copy(key_heads, keys.at[block(REACH)], own_sem.at[0])
    v_own = pltpu.make_async_copy(value_heads, values.at[block(REACH)], own_sem.at[1])
    k_own.start()
    v_own.start()

    barrier = pltpu.get_barrier_semaphore()
    for d in range(1, n_tp):
        pl.semaphore_signal(barrier, inc=1, device_id={"tp": lax.rem(t + d, n_tp)}, device_id_type=MESH)
    pl.semaphore_signal(barrier, inc=1, device_id={"ctx": partner}, device_id_type=MESH)
    for d in (2, 4):
        @pl.when(i >= d)
        def _():
            pl.semaphore_signal(barrier, inc=1, device_id={"ctx": i - d}, device_id_type=MESH)

        @pl.when(i + d < n_ctx)
        def _():
            pl.semaphore_signal(barrier, inc=1, device_id={"ctx": i + d}, device_id_type=MESH)

    def scan_doc(k, carry):
        end, first0, first1 = carry
        end = end + lengths[k]
        first0 = jnp.where(end <= 2 * i, jnp.maximum(first0, end), first0)
        first1 = jnp.where(end <= 2 * i + 1, jnp.maximum(first1, end), first1)
        return end, first0, first1

    _, first0, first1 = lax.fori_loop(0, lengths.shape[0], scan_doc, (jnp.int32(0), jnp.int32(0), jnp.int32(0)))
    lane = lax.broadcasted_iota(jnp.int32, (1, ROWS), 1)
    first = jnp.where(lane < BLK, first0, first1)
    last = jnp.where(lane < BLK, 2 * i, 2 * i + 1)
    for j in range(2 * CHUNKS):
        at = 2 * i - 2 * REACH + j
        hide[pl.ds(j, 1), :] = jnp.where((at >= first) & (at <= last), 0.0, BIG)
    for d in range(1, REACH + 1):
        @pl.when(i < d)
        def _():
            keys[block(REACH - d), :] = jnp.zeros((ROWS, HD), jnp.bfloat16)
            values[block(REACH - d), :] = jnp.zeros((ROWS, HD), jnp.bfloat16)
    dkey[...] = jnp.zeros_like(dkey)
    dvalue[...] = jnp.zeros_like(dvalue)

    partners = n_tp
    for d in (2, 4):
        partners = partners + jnp.where(i >= d, 1, 0) + jnp.where(i + d < n_ctx, 1, 0)
    pl.semaphore_wait(barrier, partners)

    def own_copy(d, what):
        src, dst, recv = ((key_heads, keys, k_recv), (value_heads, values, v_recv))[what]
        return pltpu.make_async_remote_copy(
            src_ref=src, dst_ref=dst.at[block(REACH - d)], send_sem=kv_send.at[d // 2, what],
            recv_sem=recv.at[REACH - d], device_id={"ctx": i + d}, device_id_type=MESH)

    def own_start(what):
        for d in (2, 4):
            @pl.when(i + d < n_ctx)
            def _():
                own_copy(d, what).start()

        @pl.when(even)
        def _():
            own_copy(1, what).start()

    def forward(d, to, what):
        ref, recv = ((keys, k_recv), (values, v_recv))[what]
        return pltpu.make_async_remote_copy(
            src_ref=ref.at[block(REACH - d)], dst_ref=ref.at[block(REACH - to)], send_sem=fwd_send.at[d // 2 - 1, what],
            recv_sem=recv.at[REACH - to], device_id={"ctx": partner}, device_id_type=MESH)

    def arrived(d, what):
        ref, recv = ((keys, k_recv), (values, v_recv))[what]

        @pl.when(i >= d)
        def _():
            at = ref.at[block(REACH - d)]
            pltpu.make_async_copy(at, at, recv.at[REACH - d]).wait()

    def pass_on(d, what):
        arrived(d, what)
        if d == 2:
            @pl.when((i >= d) & even)
            def _():
                forward(2, 3, what).start()

            @pl.when((i >= d) & (odd == 1))
            def _():
                forward(2, 1, what).start()
        else:
            @pl.when((i >= d) & (odd == 1))
            def _():
                forward(4, 3, what).start()

    def grad_copy(h, peer):
        return pltpu.make_async_remote_copy(
            src_ref=out_grad.at[:, pl.ds(pl.multiple_of(peer * (GROUP * HD) + h * HD, HD), HD)],
            dst_ref=grads.at[h, pl.ds(t * (ROWS // n_tp), ROWS // n_tp)],
            send_sem=g_send, recv_sem=g_recv.at[h], device_id={"tp": peer}, device_id_type=MESH)

    def grad_start(h, carry):
        for d in (4, 3, 5, 2, 6, 1, 7):
            grad_copy(h, lax.rem(t + d, n_tp)).start()
        pltpu.make_async_copy(
            out_grad.at[:, pl.ds(pl.multiple_of(t * (GROUP * HD) + h * HD, HD), HD)],
            grads.at[h, pl.ds(t * (ROWS // n_tp), ROWS // n_tp)], g_recv.at[h]).start()
        return carry

    own_start(0)
    lax.fori_loop(0, 2, grad_start, 0)
    own_start(1)
    lax.fori_loop(2, GROUP, grad_start, 0)

    pltpu.make_async_copy(q, q, q_sem).wait()
    k_own.wait()

    def scores(j, own):
        key = keys[block(j), :]
        keys_t[j] = key.T
        hide0, hide1 = hide[pl.ds(2 * j, 1), :], hide[pl.ds(2 * j + 1, 1), :]

        def some(batch, carry):
            for x in range(BATCH):
                h = batch * BATCH + x
                raw = mm(key, q[h], NT) * SCALE
                if own:
                    row_k = lax.broadcasted_iota(jnp.int32, (ROWS, ROWS), 0)
                    row_q = lax.broadcasted_iota(jnp.int32, (ROWS, ROWS), 1)
                    raw = jnp.where(row_k <= row_q, raw, -BIG)
                high0 = jnp.max(raw[:BLK], axis=0, keepdims=True) - hide0
                high1 = jnp.max(raw[BLK:], axis=0, keepdims=True) - hide1
                high = jnp.maximum(jnp.maximum(high0, high1), FLOOR)
                e0 = jnp.exp(raw[:BLK] - (high + hide0))
                e1 = jnp.exp(raw[BLK:] - (high + hide1))
                top[j, pl.ds(h, 1), :] = high
                total[j, pl.ds(h, 1), :] = jnp.sum(e0, axis=0, keepdims=True) + jnp.sum(e1, axis=0, keepdims=True)
                probs[j, :BLK, block(h)] = e0.astype(jnp.bfloat16)
                probs[j, BLK:, block(h)] = e1.astype(jnp.bfloat16)
            return carry

        lax.fori_loop(0, GROUP // BATCH, some, 0)

    scores(REACH, True)

    def far(step, carry):
        d = jnp.where(step < 2, 2 * step + 2, 2 * step - 3)
        for s, (d_k, d_v) in enumerate(((2, 0), (4, 0), (1, 2), (3, 4))):
            @pl.when(step == s)
            def _():
                pass_on(d_k, 0) if s < 2 else arrived(d_k, 0)
                if d_v:
                    pass_on(d_v, 1)
        scores(REACH - d, False)
        return carry

    lax.fori_loop(0, REACH, far, 0)

    highest = jnp.max(top[...], axis=0)
    lifted = [jnp.exp(top[j] - highest) for j in range(CHUNKS)]
    inverse = 1.0 / sum(lifted[j] * total[j] for j in range(CHUNKS))
    for j in range(CHUNKS):
        factor[j] = lifted[j] * inverse

    v_own.wait()
    arrived(1, 1)
    arrived(3, 1)
    for j in range(CHUNKS):
        values_t[j] = values[block(j), :].T

    def weigh(batch, carry):
        for x in range(2):
            h = batch * 2 + x
            out_t = jnp.zeros((HD, ROWS), jnp.float32)
            for j in range(CHUNKS):
                p = (probs[j, :, block(h)].astype(jnp.float32) * factor[j, pl.ds(h, 1), :]).astype(jnp.bfloat16)
                probs[j, :, block(h)] = p
                out_t = out_t + mm(values_t[j], p)
            outs[h] = out_t
        return carry

    lax.fori_loop(0, GROUP // 2, weigh, 0)

    def backward(pair, carry):
        heads = [2 * pair, 2 * pair + 1]
        for h in heads:
            pltpu.make_async_copy(grads.at[h], grads.at[h], g_recv.at[h]).wait()
        both = pl.ds(pl.multiple_of(pair * 2 * ROWS, 2 * ROWS), 2 * ROWS)
        grad_rows = grads[pl.ds(2 * pair, 2)].reshape(2 * ROWS, HD)
        query_rows = q[pl.ds(2 * pair, 2)].reshape(2 * ROWS, HD)
        grads_t = [grads[h].T for h in heads]
        dots = [jnp.sum(outs[h] * grads_t[x].astype(jnp.float32), axis=0, keepdims=True) for x, h in enumerate(heads)]
        dq_t = [jnp.zeros((HD, ROWS), jnp.float32) for _ in heads]
        for j in range(CHUNKS):
            ds = []
            for x, h in enumerate(heads):
                dp = mm(values[block(j), :], grads_t[x])
                ds.append(probs[j, :, block(h)] * (dp - dots[x]).astype(jnp.bfloat16))
                dq_t[x] = dq_t[x] + mm(keys_t[j], ds[x])
            dvalue[block(j), :] += mm(probs[j, :, both], grad_rows)
            dkey[block(j), :] += mm(jnp.concatenate(ds, axis=1), query_rows)
        for x, h in enumerate(heads):
            dq[:, pl.ds(pl.multiple_of(h * HD, HD), HD)] = (dq_t[x].T * SCALE).astype(jnp.bfloat16)
        return carry

    lax.fori_loop(0, GROUP // 2, backward, 0)

    def swap_copy(s):
        return pltpu.make_async_remote_copy(
            src_ref=swap.at[s], dst_ref=swapped.at[s], send_sem=swap_send.at[s], recv_sem=swap_recv.at[s],
            device_id={"ctx": partner}, device_id_type=MESH)

    def part_copy(s):
        return pltpu.make_async_remote_copy(
            src_ref=part.at[s], dst_ref=got.at[s], send_sem=part_send.at[s], recv_sem=part_recv.at[s],
            device_id={"ctx": i - 2 * (s + 1)}, device_id_type=MESH)

    def send_part(s, other):
        rows = block(REACH - 2 * (s + 1))
        key_sum, value_sum = dkey[rows, :] * SCALE, dvalue[rows, :]
        if other is not None:
            key_sum = key_sum + swapped[other, 0].astype(jnp.float32)
            value_sum = value_sum + swapped[other, 1].astype(jnp.float32)
        part[s, 0] = key_sum.astype(jnp.bfloat16)
        part[s, 1] = value_sum.astype(jnp.bfloat16)

        @pl.when(i >= 2 * (s + 1))
        def _():
            part_copy(s).start()

    for s in (1, 0):
        rows = block(REACH - (2 * s + 1))
        swap[s, 0] = (dkey[rows, :] * SCALE).astype(jnp.bfloat16)
        swap[s, 1] = dvalue[rows, :].astype(jnp.bfloat16)
        swap_copy(s).start()

    own = block(REACH)
    dkey[own, :] = dkey[own, :] * SCALE

    @pl.when(even)
    def _():
        send_part(1, None)
        swap_copy(1).wait_recv()
        send_part(0, 1)
        swap_copy(0).wait_recv()
        dkey[own, :] += swapped[0, 0].astype(jnp.float32)
        dvalue[own, :] += swapped[0, 1].astype(jnp.float32)

    @pl.when(odd == 1)
    def _():
        swap_copy(1).wait_recv()
        send_part(1, 1)
        swap_copy(0).wait_recv()
        send_part(0, 0)

    for s in (0, 1):
        @pl.when(i + 2 * (s + 1) < n_ctx)
        def _():
            part_copy(s).wait_recv()
            dkey[own, :] += got[s, 0].astype(jnp.float32)
            dvalue[own, :] += got[s, 1].astype(jnp.float32)
    dkv[0] = dkey[own, :].astype(jnp.bfloat16)
    dkv[1] = dvalue[own, :].astype(jnp.bfloat16)

    for s in (0, 1):
        swap_copy(s).wait_send()

        @pl.when(i >= 2 * (s + 1))
        def _():
            part_copy(s).wait_send()

    for what in (0, 1):
        for d in (2, 4):
            @pl.when(i + d < n_ctx)
            def _():
                own_copy(d, what).wait_send()

        @pl.when(even)
        def _():
            own_copy(1, what).wait_send()

        @pl.when(i >= 2)
        def _():
            forward(2, 1, what).wait_send()

        @pl.when((i >= 4) & (odd == 1))
        def _():
            forward(4, 3, what).wait_send()
    sent = grads.at[pl.ds(0, n_tp - 1)]
    pltpu.make_async_copy(sent, sent, g_send).wait()


def put_out(dq, dkv, dq_out, dk_out, dv_out, sems):
    copies = [pltpu.make_async_copy(dq, dq_out, sems.at[0]), pltpu.make_async_copy(dkv.at[0], dk_out, sems.at[1]),
              pltpu.make_async_copy(dkv.at[1], dv_out, sems.at[2])]
    for copy in copies:
        copy.start()
    for copy in copies:
        copy.wait()


def body(n_ctx, n_tp, queries, key_heads, value_heads, out_grad, doc_lengths):
    bf, f32 = jnp.bfloat16, jnp.float32
    any_space = pl.BlockSpec(memory_space=pl.ANY)
    vmem = pl.BlockSpec(memory_space=pltpu.VMEM)
    dma = pltpu.SemaphoreType.DMA
    dq, dkv = pl.pallas_call(
        functools.partial(kernel, n_ctx, n_tp),
        out_shape=(pltpu.VMEM((ROWS, GROUP * HD), bf), pltpu.VMEM((2, ROWS, HD), bf)),
        in_specs=[pl.BlockSpec(memory_space=pltpu.SMEM)] + [any_space] * 4,
        out_specs=[vmem] * 2,
        scratch_shapes=[
            pltpu.VMEM((GROUP, ROWS, HD), bf),
            pltpu.VMEM((CHUNKS * ROWS, HD), bf),
            pltpu.VMEM((CHUNKS * ROWS, HD), bf),
            pltpu.VMEM((CHUNKS, HD, ROWS), bf),
            pltpu.VMEM((CHUNKS, HD, ROWS), bf),
            pltpu.VMEM((GROUP, ROWS, HD), bf),
            pltpu.VMEM((CHUNKS, ROWS, GROUP * ROWS), bf),
            pltpu.VMEM((GROUP, HD, ROWS), f32),
            pltpu.VMEM((CHUNKS, GROUP, ROWS), f32),
            pltpu.VMEM((CHUNKS, GROUP, ROWS), f32),
            pltpu.VMEM((CHUNKS, GROUP, ROWS), f32),
            pltpu.VMEM((16, ROWS), f32),
            pltpu.VMEM((CHUNKS * ROWS, HD), f32),
            pltpu.VMEM((CHUNKS * ROWS, HD), f32),
            pltpu.VMEM((2, 2, ROWS, HD), bf),
            pltpu.VMEM((2, 2, ROWS, HD), bf),
            pltpu.VMEM((2, 2, ROWS, HD), bf),
            pltpu.VMEM((2, 2, ROWS, HD), bf),
            dma, dma((2,)), dma((REACH,)), dma((REACH,)), dma((3, 2)), dma((2, 2)), dma((GROUP,)), dma,
            dma((2,)), dma((2,)), dma((2,)), dma((2,)),
        ],
        compiler_params=pltpu.CompilerParams(collective_id=0, has_side_effects=True, vmem_limit_bytes=56 << 20),
    )(doc_lengths, queries, key_heads, value_heads, out_grad)
    return pl.pallas_call(
        put_out,
        out_shape=(jax.ShapeDtypeStruct(queries.shape, bf), jax.ShapeDtypeStruct(key_heads.shape, bf),
                   jax.ShapeDtypeStruct(value_heads.shape, bf)),
        in_specs=[vmem] * 2,
        out_specs=[any_space] * 3,
        scratch_shapes=[dma((3,))],
    )(pltpu.with_memory_space_constraint(dq, pltpu.VMEM), pltpu.with_memory_space_constraint(dkv, pltpu.VMEM))


def solution(mesh):
    placed = (P("ctx", "tp"), P("ctx", "tp"), P("ctx", "tp"), P(("ctx", "tp"), None), P())
    return jax.shard_map(
        functools.partial(body, mesh.shape["ctx"], mesh.shape["tp"]),
        mesh=mesh,
        in_specs=placed,
        out_specs=(P("ctx", "tp"), P("ctx", "tp"), P("ctx", "tp")),
        check_vma=False,
    )
```

time: 49.8 us -> 41.6 us (0.84)
  Pallas kernels: 45.5 us -> 40.8 us
  local copies, waits for them, and re-layouts: 3.4 us -> 0 us
    pallas_call x1 -> x2, Pallas kernels: 45.5 us -> 40.8 us  [the longest x1 39.9 us: body(): pl.pallas_call(functools.partial(kernel, n_ctx, n_tp), out_shape=(pltpu.V...]
    unnamed x7 -> x0, local copies, waits for them, and re-layouts: 3.4 us -> none
where the time goes in v2:
time: 41.6 us; the launch traced here: 41.4 us
  Pallas kernels  40.8 us (98%)
  between operations  0.64 us (2%)
    pallas_call x1, Pallas kernels, body(): pl.pallas_call(functools.partial(kernel, n_ctx, n_tp), out_shape=(pltpu.V...  39.9 us
    pallas_call x1, Pallas kernels, body(): pl.pallas_call(put_out, out_shape=(jax.ShapeDtypeStruct(queries.shape, bf...  0.85 us

profile of v2, /device:TPU:199, one launch (start us, length us, event | category | flops | bytes accessed | tf_op | source)
XLA Modules:
  0.0 41.4 jit_solution(8116768987035978891)
XLA Ops:
  0.6 39.9 %shard_map.76 = (bf16[256,1024]{1,0:T(8,128)(2,1)S(1)}, bf16[2,256,128]{2,1,0:T(8,128)(2,1)S(1)}) custom-call(s32[32]{0:T(128)} %lengths.1, bf16[256,1024]{1,0:T(8,128)(2,1)} %queries.1, bf16[256,128]{1,0:T(8,128)(2,1)} %key_heads.1, bf16[256,128]{1,0:T(8,128)(2,1)} %value_heads.1, bf16[32,8192]{1,0:T(8,128)(2,1)} %out_grad.1), custom_call_target="tpu_custom_call" | custom-call | tf_op jit(solution)/shard_map/pallas_call | solution.py:346
  40.6 0.9 %shard_map.77 = (bf16[256,1024]{1,0:T(8,128)(2,1)}, bf16[256,128]{1,0:T(8,128)(2,1)}, bf16[256,128]{1,0:T(8,128)(2,1)}) custom-call(bf16[256,1024]{1,0:T(8,128)(2,1)S(1)} %get-tuple-element.5.dq, bf16[2,256,128]{2,1,0:T(8,128)(2,1)S(1)} %get-tuple-element.6.dkv), custom_call_target="tpu_custom_call" | custom-call | tf_op jit(solution)/shard_map/pallas_call | solution.py:375
